TPU v7x, 256 devices: a whole 4x4x8 slice. The times are simulated.
256 devices in a mesh: frame: 16 (over z_hi, y), space: 16 (over z_lo, x, core).
Axes of the slice: x: 4, y: 4, z: 8 (z_hi: 4, z_lo: 2; z = z_hi * 2 + z_lo), core: 2. Of those that a mesh axis runs over, the one named last changes fastest.
Arguments:
- hidden_in: bfloat16 [2, 16, 32, 64, 1152], P(None, 'frame', 'space'), may hold values from -6 to 6
- attn_cotangent: bfloat16 [2, 16, 32, 64, 1152], P(None, 'frame', 'space'), may hold values from -6 to 6
- w_qkv: bfloat16 [1152, 3456], P('space'), may hold values from -0.1875 to 0.1875
- modulation_table: bfloat16 [1000, 2, 1152], replicated, may hold values from -3 to 3
- snr_table: float32 [1000], replicated, may hold values from 0.1 to 1
- timestep: int32 [2], replicated, may hold values from 0 to 999
- weight_index: int32 [2], replicated, may hold values from 0 to 999
Outputs:
- grad_input: bfloat16 [2, 16, 32, 64, 1152], P(None, 'frame', 'space')
- grad_w_qkv: float32 [1152, 3456], P('space')
- grad_modulation: float32 [2, 2, 1152], replicated
All inputs are finite; a program needn't handle non-finite values.
Results may differ from a plain program's by a relative error of at most 0.029.
Values may be sent and summed in bfloat16 or wider, within the bound.
A program may use at most 128 MiB of HBM per device.

v0:
```python
import jax
import jax.numpy as jnp
from jax import lax
from jax.sharding import PartitionSpec as P

HEADS = 16
HEAD_DIM = 72


def attend_back(queries, keys, values, upstream):
    factor = queries.shape[-1] ** (-0.5)
    queries = queries.astype(jnp.float32)
    keys = keys.astype(jnp.float32)
    values = values.astype(jnp.float32)
    upstream = upstream.astype(jnp.float32)
    highest = lax.Precision.HIGHEST
    scores = jnp.einsum("bfxhe,bgxhe->bxhfg", queries, keys, precision=highest) * factor
    expd = jnp.exp(scores)
    probs = expd / jnp.sum(expd, axis=-1, keepdims=True)
    grad_probs = jnp.einsum("bfxhe,bgxhe->bxhfg", upstream, values, precision=highest)
    grad_values = jnp.einsum("bxhfg,bfxhe->bgxhe", probs, upstream, precision=highest)
    grad_scores = probs * (grad_probs - jnp.sum(probs * grad_probs, axis=-1, keepdims=True))
    grad_queries = jnp.einsum("bxhfg,bgxhe->bfxhe", grad_scores, keys, precision=highest) * factor
    grad_keys = jnp.einsum("bxhfg,bfxhe->bgxhe", grad_scores, queries, precision=highest) * factor
    return (
        grad_queries.astype(jnp.bfloat16),
        grad_keys.astype(jnp.bfloat16),
        grad_values.astype(jnp.bfloat16),
    )


def per_device(
    hidden_in, attn_cotangent, w_qkv, modulation_table, snr_table, timestep, weight_index
):
    clip_count, frame_dev, row_dev, col_count, model_width = hidden_in.shape
    frame_n = lax.axis_size("frame")
    space_n = lax.axis_size("space")
    positions = row_dev * col_count
    w_full = lax.all_gather(w_qkv, "space", axis=0, tiled=True)
    both = jnp.stack(
        [
            hidden_in.reshape(clip_count, frame_dev, positions, model_width),
            attn_cotangent.reshape(clip_count, frame_dev, positions, model_width),
        ],
        axis=3,
    )
    both = lax.all_to_all(both, "frame", split_axis=2, concat_axis=1, tiled=True)
    frames = both.shape[1]
    across = both.shape[2]
    values_in = both[:, :, :, 0].astype(jnp.float32)
    average = jnp.mean(values_in, axis=-1, keepdims=True)
    centered = values_in - average
    variance = jnp.mean(centered * centered, axis=-1, keepdims=True)
    inverse_std = lax.rsqrt(variance + 1e-06)
    normed = centered * inverse_std
    modulation = modulation_table[timestep].astype(jnp.float32)
    shift = modulation[:, 0][:, None, None, :]
    scale = modulation[:, 1][:, None, None, :]
    modulated = (normed * (1.0 + scale) + shift).astype(jnp.bfloat16)
    mod_rows = modulated.reshape(-1, model_width)
    projected = jnp.dot(mod_rows, w_full, preferred_element_type=jnp.float32).astype(jnp.bfloat16)
    pieces = projected.reshape(clip_count, frames, across, 3, HEADS, HEAD_DIM)
    loss_weight = snr_table[weight_index]
    upstream = (loss_weight[:, None, None, None] * both[:, :, :, 1].astype(jnp.float32)).astype(
        jnp.bfloat16
    )
    upstream = upstream.reshape(clip_count, frames, across, HEADS, HEAD_DIM)
    head_grads = attend_back(pieces[:, :, :, 0], pieces[:, :, :, 1], pieces[:, :, :, 2], upstream)
    grad_rows = jnp.stack(head_grads, axis=3).reshape(-1, 3 * model_width)
    grad_scale_factor = float(mod_rows.shape[0] * frame_n * space_n) ** (-0.5)
    term = lax.dot_general(
        mod_rows, grad_rows, (((0,), (0,)), ((), ())), preferred_element_type=jnp.float32
    ).astype(jnp.bfloat16)
    col_blk = 3 * model_width // frame_n
    share = lax.psum_scatter(term, "space", scatter_dimension=0, tiled=True)
    share = share.reshape(share.shape[0], frame_n, col_blk)
    share = lax.psum_scatter(share, "frame", scatter_dimension=1, tiled=True)
    grad_weight = lax.all_gather(share, "frame", axis=1, tiled=True)
    grad_weight = grad_weight.reshape(share.shape[0], 3 * model_width)
    grad_weight = grad_weight.astype(jnp.float32) * grad_scale_factor
    grad_hidden = lax.dot_general(
        grad_rows, w_full, (((1,), (1,)), ((), ())), preferred_element_type=jnp.float32
    )
    grad_hidden = grad_hidden.reshape(values_in.shape)
    local_sums = jnp.stack(
        [jnp.sum(grad_hidden, axis=(1, 2)), jnp.sum(grad_hidden * normed, axis=(1, 2))], axis=1
    )
    grad_modulation = lax.psum(local_sums, ("frame", "space")) * grad_scale_factor
    grad_normed = grad_hidden * (1.0 + scale)
    grad_input = (
        grad_normed
        - jnp.mean(grad_normed, axis=-1, keepdims=True)
        - normed * jnp.mean(grad_normed * normed, axis=-1, keepdims=True)
    ) * inverse_std
    grad_input = grad_input.astype(jnp.bfloat16)
    grad_input = lax.all_to_all(grad_input, "frame", split_axis=1, concat_axis=2, tiled=True)
    grad_input = grad_input.reshape(clip_count, frame_dev, row_dev, col_count, model_width)
    return (grad_input, grad_weight, grad_modulation)


def solution(mesh):
    in_specs = (
        P(None, "frame", "space", None, None),
        P(None, "frame", "space", None, None),
        P("space", None),
        P(),
        P(),
        P(),
        P(),
    )
    out_specs = (P(None, "frame", "space", None, None), P("space", None), P())
    return jax.shard_map(
        per_device, mesh=mesh, in_specs=in_specs, out_specs=out_specs, check_vma=False
    )
```

profile of v0, /device:TPU:2, one launch (start us, length us, event | category | flops | bytes accessed | tf_op | source)
XLA Modules:
  0.0 375.7 jit_solution(3701805909269728193)
XLA Ops:
  7.9 1.7 copy.38
  9.6 1.7 copy.39
  11.3 2.7 pad_maximum_fusion.1
  13.9 11.2 %all-to-all-start = ((bf16[2,1,128,2,1152]{4,0,3,1,2:T(2,128)(2,1)}), bf16[2,1,128,2,1152]{4,0,3,1,2:T(2,128)(2,1)S(1)}, u32[]{:S(2)}, u32[]{:S(2)}) async-start(bf16[2,1,128,2,1152]{4,0,3,1,2:T(2,128)(2,1)} %pad_maximum_fusion.1), calls=%async_computation | async-start | bytes 2359296 | tf_op jit(solution)/shard_map/all_to_all | solution.py:47
  25.2 2.9 gather_fusion
  28.9 26.7 %all-to-all-done = bf16[2,1,128,2,1152]{4,0,3,1,2:T(2,128)(2,1)S(1)} async-done(((bf16[2,1,128,2,1152]{4,0,3,1,2:T(2,128)(2,1)}), bf16[2,1,128,2,1152]{4,0,3,1,2:T(2,128)(2,1)S(1)}, u32[]{:S(2)}, u32[]{:S(2)}) %all-to-all-start) | async-done | bytes 1179680 | tf_op jit(solution)/shard_map/all_to_all | solution.py:47
  56.4 3.1 reshape.157
  59.9 28.9 %all-gather.2.cloned.1.call-done = bf16[1152,3456]{1,0:T(8,128)(2,1)} async-done(((bf16[72,3456]{1,0:T(8,128)(2,1)}), bf16[1152,3456]{1,0:T(8,128)(2,1)}) %all-gather.2.cloned.1.call-update) | async-done | bytes 7962640 | tf_op jit(solution)/shard_map/all_gather | solution.py:39
  88.8 7.0 %convolution_convert_fusion.1 = bf16[256,3456]{1,0:T(8,128)(2,1)} fusion(bf16[256,1152]{1,0:T(8,128)(2,1)S(1)} %fusion.8, bf16[1152,3456]{1,0:T(8,128)(2,1)} %all-gather.2.cloned.1.call-done), kind=kOutput, calls=%fused_computation.5 | convolution fusion | flops 2039316480 | bytes 10321920 | tf_op jit(solution)/shard_map/dot_general | solution.py:61
  95.8 7.1 %reshape.152 = bf16[2,16,8,3,16,72]{5,4,3,2,1,0:T(8,128)(2,1)S(1)} reshape(bf16[256,3456]{1,0:T(8,128)(2,1)} %convolution_convert_fusion.1) | data formatting | bytes 3538944 | tf_op jit(solution)/shard_map/reshape | solution.py:62
  102.9 0.9 fusion.18
  103.9 1.7 fusion.4
  105.6 2.3 multiply_reduce_fusion
  107.9 2.4 fusion.6
  110.3 2.2 fusion.7
  112.6 2.8 fusion.5
  116.1 0.8 copy.46
  116.9 4.6 %dot_general.32 = bf16[2,16,8,3456]{3,2,1,0:T(8,128)(2,1)} reshape(bf16[2,16,8,3,16,72]{5,4,3,2,1,0:T(8,128)(2,1)S(1)} %copy.46) | data formatting | bytes 3538944 | tf_op jit(solution)/shard_map/dot_general | solution.py:81
  121.5 4.6 %reshape.154 = bf16[256,3456]{1,0:T(8,128)(2,1)} reshape(bf16[2,16,8,3,16,72]{5,4,3,2,1,0:T(8,128)(2,1)S(1)} %copy.46) | data formatting | bytes 3538944 | tf_op jit(solution)/shard_map/reshape | solution.py:69
  126.1 6.7 %multiply_reduce_fusion.1 = (f32[2,1152]{1,0:T(2,128)S(1)}, f32[2,16,8]{2,1,0:T(8,128)S(1)}, f32[2,16,8]{2,1,0:T(8,128)S(1)}, f32[2,1152]{1,0:T(2,128)S(1)}, bf1...) fusion(f32[2,16,8]{2,1,0:T(8,128)S(1)} %add_rsqrt_fusion, ...), kind=kOutput, calls=%fused_computation.28 | convolution fusion | flops 2042260480 | bytes 12132352 | tf_op jit(solution)/shard_map/dot_general | solution.py:81
  132.8 5.4 %convolution_convert_fusion = bf16[1152,3456]{1,0:T(8,128)(2,1)} fusion(bf16[256,1152]{1,0:T(8,128)(2,1)S(1)} %bitcast.101, bf16[256,3456]{1,0:T(8,128)(2,1)S(1)} %copy-done.3), kind=kOutput, calls=%fused_computation.2 | convolution fusion | flops 2042413056 | bytes 10321920 | tf_op jit(solution)/shard_map/dot_general | solution.py:71
  138.3 1.2 copy-done.2
  140.0 0.9 copy.47
  140.8 8.8 %all-to-all-start.1 = ((bf16[2,16,8,1152]{3,2,0,1:T(8,128)(2,1)}), bf16[2,16,8,1152]{3,2,0,1:T(8,128)(2,1)S(1)}, u32[]{:S(2)}, u32[]{:S(2)}) async-start(bf16[2,16,8,1152]{3,2,0,1:T(8,128)(2,1)} %copy.47), calls=%async_computation.1 | async-start | bytes 1179648 | tf_op jit(solution)/shard_map/all_to_all | solution.py:96
  149.7 76.9 %reduce-scatter.8.cloned.1.call-done = bf16[72,3456]{1,0:T(8,128)(2,1)} async-done(((bf16[1152,3456]{1,0:T(8,128)(2,1)}), bf16[72,3456]{1,0:T(8,128)(2,1)}) %reduce-scatter.8.cloned.1.call-update) | async-done | bytes 497680
  226.6 2.8 reshape.155
  229.3 1.0 copy.50
  230.4 80.8 %psum.7 = f32[2,2,1152]{2,0,1:T(2,128)S(1)} all-reduce(f32[2,2,1152]{2,0,1:T(2,128)S(1)} %pad_maximum_fusion.2), channel_id=1, replica_groups=mesh['frame'=16,'space'=16] {'frame','space'}, use_global_device_ids=true, to_apply=%region_10.0 | all-reduce | flops 4608 | bytes 36864 | tf_op jit(solution)/shard_map/psum | solution.py:88
  311.8 0.9 copy.48
  312.6 8.1 %reduce-scatter.6.cloned.1.call-done = bf16[72,1,216]{2,0,1:T(8,128)(2,1)} async-done(((bf16[72,16,216]{2,0,1:T(8,128)(2,1)}), bf16[72,1,216]{2,0,1:T(8,128)(2,1)}) %reduce-scatter.6.cloned.1.call-update) | async-done | bytes 31120 | tf_op jit(solution)/shard_map/reduce_scatter | solution.py:77
  320.8 46.3 %all_gather.7 = bf16[72,16,216]{2,0,1:T(8,128)(2,1)S(1)} all-gather(bf16[72,1,216]{2,0,1:T(8,128)(2,1)} %reduce-scatter.6.cloned.1.call-done), channel_id=1, replica_groups=mesh['frame'=16,'space'=16] {'frame'}, dimensions={1}, use_global_device_ids=true | all-gather | bytes 528768 | tf_op jit(solution)/shard_map/all_gather | solution.py:78
  367.5 1.6 mul.137
  (47 shorter events, 5.0 us)
Async XLA Ops:
  7.2 21.0 %copy-start = (f32[1000]{0:T(1024)S(1)}, f32[1000]{0:T(1024)}, u32[]{:S(2)}) copy-start(f32[1000]{0:T(1024)} %param.11) | copy-start | bytes 12004
  7.2 81.6 %all-gather.2.cloned.1.call-start = ((), (), s32[]{:S(2)}) async-start(), calls=%async_computation.4 | async-start | bytes 8460288 | tf_op jit(solution)/shard_map/all_gather | solution.py:39
  11.3 13.9 %copy-start.5 = (s32[2]{0:T(128)S(1)}, s32[2]{0:T(128)}, u32[]{:S(2)}) copy-start(s32[2]{0:T(128)} %param.12) | copy-start | bytes 28
  11.3 16.9 %copy-start.6 = (s32[2]{0:T(128)S(1)}, s32[2]{0:T(128)}, u32[]{:S(2)}) copy-start(s32[2]{0:T(128)} %param.13) | copy-start | bytes 28
  13.9 41.6 %all-to-all-start = ((bf16[2,1,128,2,1152]{4,0,3,1,2:T(2,128)(2,1)}), bf16[2,1,128,2,1152]{4,0,3,1,2:T(2,128)(2,1)S(1)}, u32[]{:S(2)}, u32[]{:S(2)}) async-start(bf16[2,1,128,2,1152]{4,0,3,1,2:T(2,128)(2,1)} %pad_maximum_fusion.1), calls=%async_computation | async-start | bytes 2359296 | tf_op jit(solution)/shard_map/all_to_all | solution.py:47
  25.2 201.4 %reduce-scatter.8.cloned.1.call-start = ((), (), s32[]{:S(2)}) async-start(), calls=%async_computation.6 | async-start | bytes 8460288
  55.7 3.9 %copy-start.1 = (bf16[2,1,128,2,1152]{4,2,0,3,1:T(8,128)(2,1)}, bf16[2,1,128,2,1152]{4,2,0,3,1:T(8,128)(2,1)S(1)}, u32[]{:S(2)}) copy-start(bf16[2,1,128,2,1152]{4,2,0,3,1:T(8,128)(2,1)S(1)} %copy.85) | copy-start | bytes 3538948
  103.9 1.7 copy-start.4
  126.1 6.7 %copy-start.3 = (bf16[256,3456]{1,0:T(8,128)(2,1)S(1)}, bf16[256,3456]{1,0:T(8,128)(2,1)}, u32[]{:S(2)}) copy-start(bf16[256,3456]{1,0:T(8,128)(2,1)} %reshape.154) | copy-start | bytes 5308420
  138.3 1.3 copy-start.2
  140.8 170.9 %all-to-all-start.1 = ((bf16[2,16,8,1152]{3,2,0,1:T(8,128)(2,1)}), bf16[2,16,8,1152]{3,2,0,1:T(8,128)(2,1)S(1)}, u32[]{:S(2)}, u32[]{:S(2)}) async-start(bf16[2,16,8,1152]{3,2,0,1:T(8,128)(2,1)} %copy.47), calls=%async_computation.1 | async-start | bytes 1179648 | tf_op jit(solution)/shard_map/all_to_all | solution.py:96
  149.6 171.1 %reduce-scatter.6.cloned.1.call-start = ((), (), s32[]{:S(2)}) async-start(), calls=%async_computation.5 | async-start | bytes 626688 | tf_op jit(solution)/shard_map/reduce_scatter | solution.py:77
Sparse Core Ops, SparseCore 0:
  9.9 78.8 all-gather.1
  138.4 88.0 reduce-scatter.7
  230.6 90.0 reduce-scatter.5
where the time goes:
time: 376 us
  waiting for transfers between devices  141 us (38%)
  blocking collectives  127 us (34%)
  local copies, waits for them, and re-layouts  37.7 us (10%)
  matrix products  30.6 us (8%)
  starting transfers between devices  20.1 us (5%)
  between operations  14.1 us (4%)
  other arithmetic  4.83 us (1%)
    psum x1, blocking collectives, per_device(): lax.psum(local_sums, ('frame', 'space')) * grad_scale_factor  80.8 us
    unnamed x4, waiting for transfers between devices  77.6 us
    all_gather x1, blocking collectives, per_device(): grad_weight = lax.all_gather(share, 'frame', axis=1, tiled=True)  46.3 us
    all_gather x1, waiting for transfers between devices, per_device(): w_full = lax.all_gather(w_qkv, 'space', axis=0, tiled=True)  28.9 us
    all_to_all x1, waiting for transfers between devices, per_device(): lax.all_to_all(both, 'frame', split_axis=2, concat_axis=1, tiled=True)  26.7 us
    all_to_all x1, starting transfers between devices, per_device(): lax.all_to_all(both, 'frame', split_axis=2, concat_axis=1, tiled=True)  11.2 us
    all_to_all x1, starting transfers between devices, per_device(): lax.all_to_all(grad_input, 'frame', split_axis=1, concat_axis=2, tiled=True)  8.77 us
    reduce_scatter x1, waiting for transfers between devices, per_device(): share = lax.psum_scatter(share, 'frame', scatter_dimension=1, tiled=True)  8.13 us
  transfers between devices with their start and end apart: 5, of which 4 were waited for; matrix products, arithmetic and copies ran while one was open for 5% of the time, Pallas kernels for 0%

commit v1 on v0

--- a/solution.py
+++ b/solution.py
@@ -75,7 +75,9 @@
     share = lax.psum_scatter(term, "space", scatter_dimension=0, tiled=True)
     share = share.reshape(share.shape[0], frame_n, col_blk)
     share = lax.psum_scatter(share, "frame", scatter_dimension=1, tiled=True)
-    grad_weight = lax.all_gather(share, "frame", axis=1, tiled=True)
+    grad_weight = jnp.concatenate(
+        lax.all_to_all(jnp.stack([share] * lax.axis_size("frame")), "frame", 0, 0), axis=1
+    )
     grad_weight = grad_weight.reshape(share.shape[0], 3 * model_width)
     grad_weight = grad_weight.astype(jnp.float32) * grad_scale_factor
     grad_hidden = lax.dot_general(

time: 376 us -> 417 us (1.11)
  waiting for transfers between devices: 141 us -> 224 us
  blocking collectives: 127 us -> 76.5 us
  starting transfers between devices: 20.1 us -> 25.9 us
    reduce_scatter x1, waiting for transfers between devices: 8.13 us -> 90.4 us  [per_device(): share = lax.psum_scatter(share, 'frame', scatter_dimension=1, tiled=True)]
    all_gather x1 -> x0, blocking collectives: 46.3 us -> none  [per_device(): grad_weight = lax.all_gather(share, 'frame', axis=1, tiled=True)]
    all_to_all x0 -> x1, starting transfers between devices: none -> 5.85 us  [per_device(): lax.all_to_all(jnp.stack([share] * lax.axis_size('frame')), 'frame', 0, 0)]
    psum x1, blocking collectives: 80.8 us -> 76.5 us  [per_device(): lax.psum(local_sums, ('frame', 'space')) * grad_scale_factor]
  transfers between devices with their start and end apart: 5 -> 6, of which waited for: 4 -> 4; matrix products, arithmetic and copies ran while one was open for 5% -> 5% of each run, Pallas kernels for 0% -> 0%
where the time goes in v1:
time: 417 us; the launch traced here: 415 us
  waiting for transfers between devices  224 us (54%)
  blocking collectives  76.5 us (18%)
  local copies, waits for them, and re-layouts  39.4 us (9%)
  matrix products  30.6 us (7%)
  starting transfers between devices  25.9 us (6%)
  between operations  14.1 us (3%)
  other arithmetic  4.83 us (1%)
    reduce_scatter x1, waiting for transfers between devices, per_device(): share = lax.psum_scatter(share, 'frame', scatter_dimension=1, tiled=True)  90.4 us
    unnamed x4, waiting for transfers between devices  77.6 us
    psum x1, blocking collectives, per_device(): lax.psum(local_sums, ('frame', 'space')) * grad_scale_factor  76.5 us
    all_gather x1, waiting for transfers between devices, per_device(): w_full = lax.all_gather(w_qkv, 'space', axis=0, tiled=True)  28.9 us
    all_to_all x1, waiting for transfers between devices, per_device(): lax.all_to_all(both, 'frame', split_axis=2, concat_axis=1, tiled=True)  26.7 us
    all_to_all x1, starting transfers between devices, per_device(): lax.all_to_all(both, 'frame', split_axis=2, concat_axis=1, tiled=True)  11.2 us
    all_to_all x1, starting transfers between devices, per_device(): lax.all_to_all(grad_input, 'frame', split_axis=1, concat_axis=2, tiled=True)  8.77 us
  transfers between devices with their start and end apart: 6, of which 4 were waited for; matrix products, arithmetic and copies ran while one was open for 5% of the time, Pallas kernels for 0%

profile of v1, /device:TPU:2, one launch (start us, length us, event | category | flops | bytes accessed | tf_op | source)
XLA Modules:
  0.0 414.9 jit_solution(17517000707990849442)
XLA Ops:
  7.9 1.7 copy.53
  9.6 1.7 copy.54
  11.3 2.7 pad_maximum_fusion.1
  13.9 11.2 %all-to-all-start = ((bf16[2,1,128,2,1152]{4,0,3,1,2:T(2,128)(2,1)}), bf16[2,1,128,2,1152]{4,0,3,1,2:T(2,128)(2,1)S(1)}, u32[]{:S(2)}, u32[]{:S(2)}) async-start(bf16[2,1,128,2,1152]{4,0,3,1,2:T(2,128)(2,1)} %pad_maximum_fusion.1), calls=%async_computation | async-start | bytes 2359296 | tf_op jit(solution)/shard_map/all_to_all | solution.py:47
  25.2 2.9 gather_fusion
  28.9 26.7 %all-to-all-done = bf16[2,1,128,2,1152]{4,0,3,1,2:T(2,128)(2,1)S(1)} async-done(((bf16[2,1,128,2,1152]{4,0,3,1,2:T(2,128)(2,1)}), bf16[2,1,128,2,1152]{4,0,3,1,2:T(2,128)(2,1)S(1)}, u32[]{:S(2)}, u32[]{:S(2)}) %all-to-all-start) | async-done | bytes 1179680 | tf_op jit(solution)/shard_map/all_to_all | solution.py:47
  56.4 3.1 reshape.160
  59.9 28.9 %all-gather.2.cloned.1.call-done = bf16[1152,3456]{1,0:T(8,128)(2,1)} async-done(((bf16[72,3456]{1,0:T(8,128)(2,1)}), bf16[1152,3456]{1,0:T(8,128)(2,1)}) %all-gather.2.cloned.1.call-update) | async-done | bytes 7962640 | tf_op jit(solution)/shard_map/all_gather | solution.py:39
  88.8 7.0 %convolution_convert_fusion.1 = bf16[256,3456]{1,0:T(8,128)(2,1)} fusion(bf16[256,1152]{1,0:T(8,128)(2,1)S(1)} %fusion.8, bf16[1152,3456]{1,0:T(8,128)(2,1)} %all-gather.2.cloned.1.call-done), kind=kOutput, calls=%fused_computation.5 | convolution fusion | flops 2039316480 | bytes 10321920 | tf_op jit(solution)/shard_map/dot_general | solution.py:61
  95.8 7.1 %reshape.155 = bf16[2,16,8,3,16,72]{5,4,3,2,1,0:T(8,128)(2,1)S(1)} reshape(bf16[256,3456]{1,0:T(8,128)(2,1)} %convolution_convert_fusion.1) | data formatting | bytes 3538944 | tf_op jit(solution)/shard_map/reshape | solution.py:62
  102.9 0.9 fusion.18
  103.9 1.7 fusion.4
  105.6 2.3 multiply_reduce_fusion
  107.9 2.4 fusion.6
  110.3 2.2 fusion.7
  112.6 2.8 fusion.5
  116.9 4.6 %dot_general.32 = bf16[2,16,8,3456]{3,2,1,0:T(8,128)(2,1)} reshape(bf16[2,16,8,3,16,72]{5,4,3,2,1,0:T(8,128)(2,1)S(1)} %copy.61) | data formatting | bytes 3538944 | tf_op jit(solution)/shard_map/dot_general | solution.py:83
  121.5 4.6 %reshape.157 = bf16[256,3456]{1,0:T(8,128)(2,1)} reshape(bf16[2,16,8,3,16,72]{5,4,3,2,1,0:T(8,128)(2,1)S(1)} %copy.61) | data formatting | bytes 3538944 | tf_op jit(solution)/shard_map/reshape | solution.py:69
  126.1 6.7 %multiply_reduce_fusion.1 = (f32[2,1152]{1,0:T(2,128)S(1)}, f32[2,16,8]{2,1,0:T(8,128)S(1)}, f32[2,16,8]{2,1,0:T(8,128)S(1)}, f32[2,1152]{1,0:T(2,128)S(1)}, bf1...) fusion(f32[2,16,8]{2,1,0:T(8,128)S(1)} %add_rsqrt_fusion, ...), kind=kOutput, calls=%fused_computation.28 | convolution fusion | flops 2042260480 | bytes 12132352 | tf_op jit(solution)/shard_map/dot_general | solution.py:83
  132.8 5.4 %convolution_convert_fusion = bf16[1152,3456]{1,0:T(8,128)(2,1)} fusion(bf16[256,1152]{1,0:T(8,128)(2,1)S(1)} %bitcast.108, bf16[256,3456]{1,0:T(8,128)(2,1)S(1)} %copy-done.3), kind=kOutput, calls=%fused_computation.2 | convolution fusion | flops 2042413056 | bytes 10321920 | tf_op jit(solution)/shard_map/dot_general | solution.py:71
  138.3 1.2 copy-done.2
  140.0 0.9 copy.62
  140.8 8.8 %all-to-all-start.1 = ((bf16[2,16,8,1152]{3,2,0,1:T(8,128)(2,1)}), bf16[2,16,8,1152]{3,2,0,1:T(8,128)(2,1)S(1)}, u32[]{:S(2)}, u32[]{:S(2)}) async-start(bf16[2,16,8,1152]{3,2,0,1:T(8,128)(2,1)} %copy.62), calls=%async_computation.1 | async-start | bytes 1179648 | tf_op jit(solution)/shard_map/all_to_all | solution.py:98
  149.7 76.9 %reduce-scatter.8.cloned.1.call-done = bf16[72,3456]{1,0:T(8,128)(2,1)} async-done(((bf16[1152,3456]{1,0:T(8,128)(2,1)}), bf16[72,3456]{1,0:T(8,128)(2,1)}) %reduce-scatter.8.cloned.1.call-update) | async-done | bytes 497680
  226.6 2.8 reshape.158
  229.3 1.0 copy.65
  230.4 90.4 %reduce-scatter.6.cloned.1.call-done = bf16[72,1,216]{2,0,1:T(8,128)(2,1)} async-done(((bf16[72,16,216]{2,0,1:T(8,128)(2,1)}), bf16[72,1,216]{2,0,1:T(8,128)(2,1)}) %reduce-scatter.6.cloned.1.call-update) | async-done | bytes 31120 | tf_op jit(solution)/shard_map/reduce_scatter | solution.py:77
  320.8 1.6 stack.23
  322.4 5.9 %all-to-all-start.2 = ((bf16[16,72,1,216]{3,1,2,0:T(8,128)(2,1)}), bf16[16,72,1,216]{3,1,2,0:T(8,128)(2,1)S(1)}, u32[]{:S(2)}, u32[]{:S(2)}) async-start(bf16[16,72,1,216]{3,1,2,0:T(8,128)(2,1)} %stack.23), calls=%async_computation.3 | async-start | bytes 1179648 | tf_op jit(solution)/shard_map/all_to_all | solution.py:79
  328.3 76.5 %psum.7 = f32[2,2,1152]{2,0,1:T(2,128)S(1)} all-reduce(f32[2,2,1152]{2,0,1:T(2,128)S(1)} %pad_maximum_fusion.2), channel_id=1, replica_groups=mesh['frame'=16,'space'=16] {'frame','space'}, use_global_device_ids=true, to_apply=%region_10.0 | all-reduce | flops 4608 | bytes 36864 | tf_op jit(solution)/shard_map/psum | solution.py:90
  405.4 0.9 copy.63
  406.7 1.6 mul.141
  (49 shorter events, 5.8 us)
Async XLA Ops:
  7.2 21.0 %copy-start = (f32[1000]{0:T(1024)S(1)}, f32[1000]{0:T(1024)}, u32[]{:S(2)}) copy-start(f32[1000]{0:T(1024)} %param.11) | copy-start | bytes 12004
  7.2 81.6 %all-gather.2.cloned.1.call-start = ((), (), s32[]{:S(2)}) async-start(), calls=%async_computation.5 | async-start | bytes 8460288 | tf_op jit(solution)/shard_map/all_gather | solution.py:39
  11.3 13.9 %copy-start.5 = (s32[2]{0:T(128)S(1)}, s32[2]{0:T(128)}, u32[]{:S(2)}) copy-start(s32[2]{0:T(128)} %param.12) | copy-start | bytes 28
  11.3 16.9 %copy-start.6 = (s32[2]{0:T(128)S(1)}, s32[2]{0:T(128)}, u32[]{:S(2)}) copy-start(s32[2]{0:T(128)} %param.13) | copy-start | bytes 28
  13.9 41.6 %all-to-all-start = ((bf16[2,1,128,2,1152]{4,0,3,1,2:T(2,128)(2,1)}), bf16[2,1,128,2,1152]{4,0,3,1,2:T(2,128)(2,1)S(1)}, u32[]{:S(2)}, u32[]{:S(2)}) async-start(bf16[2,1,128,2,1152]{4,0,3,1,2:T(2,128)(2,1)} %pad_maximum_fusion.1), calls=%async_computation | async-start | bytes 2359296 | tf_op jit(solution)/shard_map/all_to_all | solution.py:47
  25.2 201.4 %reduce-scatter.8.cloned.1.call-start = ((), (), s32[]{:S(2)}) async-start(), calls=%async_computation.7 | async-start | bytes 8460288
  55.7 3.9 copy-start.1
  103.9 1.7 copy-start.4
  126.1 6.7 %copy-start.3 = (bf16[256,3456]{1,0:T(8,128)(2,1)S(1)}, bf16[256,3456]{1,0:T(8,128)(2,1)}, u32[]{:S(2)}) copy-start(bf16[256,3456]{1,0:T(8,128)(2,1)} %reshape.157) | copy-start | bytes 5308420
  138.3 1.3 copy-start.2
  140.8 89.5 %all-to-all-start.1 = ((bf16[2,16,8,1152]{3,2,0,1:T(8,128)(2,1)}), bf16[2,16,8,1152]{3,2,0,1:T(8,128)(2,1)S(1)}, u32[]{:S(2)}, u32[]{:S(2)}) async-start(bf16[2,16,8,1152]{3,2,0,1:T(8,128)(2,1)} %copy.62), calls=%async_computation.1 | async-start | bytes 1179648 | tf_op jit(solution)/shard_map/all_to_all | solution.py:98
  149.6 171.1 %reduce-scatter.6.cloned.1.call-start = ((), (), s32[]{:S(2)}) async-start(), calls=%async_computation.6 | async-start | bytes 626688 | tf_op jit(solution)/shard_map/reduce_scatter | solution.py:77
  322.4 83.9 %all-to-all-start.2 = ((bf16[16,72,1,216]{3,1,2,0:T(8,128)(2,1)}), bf16[16,72,1,216]{3,1,2,0:T(8,128)(2,1)S(1)}, u32[]{:S(2)}, u32[]{:S(2)}) async-start(bf16[16,72,1,216]{3,1,2,0:T(8,128)(2,1)} %stack.23), calls=%async_computation.3 | async-start | bytes 1179648 | tf_op jit(solution)/shard_map/all_to_all | solution.py:79
Sparse Core Ops, SparseCore 0:
  9.9 78.8 all-gather.1
  138.4 88.0 reduce-scatter.7
  230.6 90.0 reduce-scatter.5
